TPU v7x, 128 devices: a whole 4x4x4 slice. The times are simulated.
128 devices in a mesh: dp: 8 (over y_lo, z), ctx: 16 (over y_hi, x, core).
Axes of the slice: x: 4, y: 4 (y_hi: 2, y_lo: 2; y = y_hi * 2 + y_lo), z: 4, core: 2. Of those that a mesh axis runs over, the one named last changes fastest.
Arguments:
- queries: bfloat16 [65536, 2048], P(('dp', 'ctx')), parts along dimension 0, may hold values from -72 to 72
- key_rows: bfloat16 [65536, 1024], P(('dp', 'ctx')), parts along dimension 0, may hold values from -6 to 6
- value_rows: bfloat16 [65536, 1024], P(('dp', 'ctx')), parts along dimension 0, may hold values from -6 to 6
- parents: int32 [512], P('dp'), parts along dimension 0, may hold values from 0 to 62, as said below
- kept_tiles: int32 [512], P('dp'), parts along dimension 0, may hold values from 0 to 1, as said below
Outputs:
- attended: bfloat16 [65536, 2048], P(('dp', 'ctx')), parts along dimension 0
There are 8 independent parts, one for each index of `dp`. A program takes and returns all parts, laid end to end along the dimension named above; each array names one. Nothing has to cross between parts.
Inputs may be any that keep to these rules, and one draw needn't show every extreme that they name: parents[b] is one to three less than b for b > 0, and parents[0] = 0. `kept_tiles`: 1 keeps a tile of 128 positions, 0 prunes it; the tiles of one index of ctx keep at most 2 tiles, and some such shard keeps exactly that many.
All inputs are finite; a program needn't handle non-finite values.
Results may differ from a plain program's by a relative error of at most 0.0065.
Values may be sent and summed in bfloat16 or wider, within the bound.
A program may use at most 576 MiB of HBM per device.

v0:
```python
import jax
import jax.numpy as jnp
from jax import lax
from jax.sharding import PartitionSpec as P

HEADS = 16
KV_HEADS = 8
HEAD_DIM = 128
WINDOW = 4096
BLK = 128


score_scale = 1.0 / 12.0


def passed_along(value, axis, by):
    length = lax.axis_size(axis)
    pairs = [(i, i + by) for i in range(length) if 0 <= i + by < length]
    return lax.ppermute(value, axis, pairs)


def ancestry(parents, kept_tiles):
    count_tiles = parents.shape[0]
    block_index = jnp.arange(count_tiles, dtype=jnp.int32)

    def advance(turn, carried):
        current, reached = carried
        onehot = current[:, None] == block_index[None, :]
        current = jnp.sum(jnp.where(onehot, parents[None, :], 0), axis=1)
        reached = jnp.logical_or(reached, current[:, None] == block_index[None, :])
        return (current, reached)

    start_reach = block_index[:, None] == block_index[None, :]
    _, reached = lax.fori_loop(0, WINDOW // BLK, advance, (block_index, start_reach))
    kept = kept_tiles > 0
    return reached & kept[:, None] & kept[None, :]


def body(queries, key_rows, value_rows, parents, kept_tiles):
    row_count = queries.shape[0]
    groups = HEADS // KV_HEADS
    count_tiles = parents.shape[0]
    my_index = lax.axis_index("ctx")
    own_start = my_index * row_count
    query_heads = queries.reshape(row_count, KV_HEADS, groups, HEAD_DIM)
    visible = ancestry(parents, kept_tiles).astype(jnp.float32)
    block_index = jnp.arange(count_tiles, dtype=jnp.int32)
    query_place = own_start + jnp.arange(row_count, dtype=jnp.int32)
    query_onehot = ((query_place // BLK)[:, None] == block_index[None, :]).astype(jnp.float32)
    query_reach = jnp.dot(query_onehot, visible, preferred_element_type=jnp.float32)

    def attend(running, pieces, key_place):
        piece_keys, piece_values = pieces
        piece_rows = piece_keys.shape[0]
        key_block = jnp.clip(key_place, 0, count_tiles * BLK - 1) // BLK
        key_onehot = (key_block[:, None] == block_index[None, :]).astype(jnp.float32)
        allowed = jnp.dot(query_reach, key_onehot.T, preferred_element_type=jnp.float32) > 0.5
        allowed = allowed & (key_place[None, :] >= 0) & (key_place[None, :] <= query_place[:, None])
        allowed = allowed & (query_place[:, None] - key_place[None, :] < WINDOW)
        running_max, row_total, weighted = running
        key_heads = piece_keys.reshape(piece_rows, KV_HEADS, HEAD_DIM)
        value_heads = piece_values.reshape(piece_rows, KV_HEADS, HEAD_DIM)
        scores = (
            jnp.einsum("qhgd,khd->hgqk", query_heads, key_heads, preferred_element_type=jnp.float32)
            * score_scale
        )
        masked = jnp.where(allowed, scores, -1e30)
        new_max = jnp.maximum(running_max, jnp.max(masked, axis=-1))
        rescale = jnp.exp(running_max - new_max)
        exp_terms = jnp.where(allowed, jnp.exp(scores - new_max[..., None]), 0.0)
        row_total = row_total * rescale + jnp.sum(exp_terms, axis=-1)
        weights = exp_terms.astype(jnp.bfloat16)
        weighted = weighted * rescale[..., None] + jnp.einsum(
            "hgqk,khd->hgqd", weights, value_heads, preferred_element_type=jnp.float32
        )
        return (new_max, row_total, weighted)

    def attend_from(running, pieces, key_start):
        key_place = key_start + jnp.arange(pieces[0].shape[0], dtype=jnp.int32)
        return attend(running, pieces, key_place)

    running = (
        jnp.full((KV_HEADS, groups, row_count), -1e30, jnp.float32),
        jnp.zeros((KV_HEADS, groups, row_count), jnp.float32),
        jnp.zeros((KV_HEADS, groups, row_count, HEAD_DIM), jnp.float32),
    )
    running = attend_from(running, (key_rows, value_rows), own_start)
    reach_depth = min(-(-WINDOW // row_count), lax.axis_size("ctx") - 1)
    stacked = jnp.stack([key_rows, value_rows])
    for hop_index in range(1, reach_depth + 1):
        arrived = passed_along(stacked, "ctx", hop_index)
        running = attend_from(running, (arrived[0], arrived[1]), own_start - hop_index * row_count)
    running_max, row_total, weighted = running
    safe_total = jnp.where(row_total > 0, row_total, 1.0)
    result = jnp.where(row_total[..., None] > 0, weighted / safe_total[..., None], 0.0)
    return result.transpose(2, 0, 1, 3).reshape(row_count, HEADS * HEAD_DIM).astype(jnp.bfloat16)


def solution(mesh):
    return jax.shard_map(
        body,
        mesh=mesh,
        in_specs=(
            P(("dp", "ctx"), None),
            P(("dp", "ctx"), None),
            P(("dp", "ctx"), None),
            P("dp"),
            P("dp"),
        ),
        out_specs=P(("dp", "ctx"), None),
        check_vma=False,
    )
```

profile of v0, /device:TPU:1, one launch (start us, length us, event | category | flops | bytes accessed | tf_op | source)
XLA Modules:
  0.0 590.6 jit_solution(15735143554627995890)
XLA Ops:
  4.9 7.4 %collective-permute-start.2 = (bf16[2,512,1024]{1,2,0:T(8,128)(2,1)}, bf16[2,512,1024]{1,2,0:T(8,128)(2,1)}, u32[]{:S(2)}, u32[]{:S(2)}) collective-permute-start(bf16[2,512,1024]{1,2,0:T(8,128)(2,1)} %pad_maximum_fusion), channel_id=1, source_target_pairs={{0,3},{1,4},{2,5},{3,6},{4,7},{5,8},{6,9},{7,10},{8,11},{9,12},{10... | collective-permute-start | bytes 6291464 | tf_op jit(solution)/shard_map/ppermute | solution.py:19
  25.2 30.7 %while.14 = (s32[]{:T(128)}, s32[64]{0:T(128)S(1)}, pred[64,64]{1,0:T(32,128)(4,1)S(1)}, s32[64]{0:T(128)}, s32[]{:T(128)}) while((s32[]{:T(128)}, s32[64]{0:T(128)S(1)}, pred[64,64]{1,0:T(32,128)(4,1)S(1)}, s32[64]{0:T(128)}, s32[]{:T(128)}) %tuple.69), condition=%wide.region_2.3_spmd.clone.clone, body=%wide.region_0.2_spmd.clone.clone.sunk | while | flops 20418 | bytes 9789 | solution.py:34
  82.0 8.7 %fusion.27 = (f32[8,2,512]{2,1,0:T(2,128)S(1)}, f32[8,512,512,2]{2,1,3,0:T(8,128)}) fusion(pred[512,512]{0,1:T(8,128)(4,1)} %copy.44, bf16[512,8,2,128]{3,2,1,0:T(2,128)(2,1)S(1)} %reshape.589, bf16[512,8,128,1]{2,1,0,3:T(8,128)(2,1)S(1)} %bitcast.464), kind=kOutput, calls=%fused_computation.47 | convolution fusion | flops 1086316544 | bytes 20217856 | tf_op jit(solution)/shard_map/qhgd,khd->hgqk/dot_general | solution.py:64
  90.7 12.4 %collective-permute-start.3 = (bf16[2,512,1024]{1,2,0:T(8,128)(2,1)}, bf16[2,512,1024]{1,2,0:T(8,128)(2,1)S(1)}, u32[]{:S(2)}, u32[]{:S(2)}) collective-permute-start(bf16[2,512,1024]{1,2,0:T(8,128)(2,1)} %pad_maximum_fusion), channel_id=1, source_target_pairs={{0,4},{1,5},{2,6},{3,7},{4,8},{5,9},{6,10},{7,11},{8,12},{9,13},{1... | collective-permute-start | bytes 6291464 | tf_op jit(solution)/shard_map/ppermute | solution.py:19
  110.0 196.1 %collective-permute-done.7 = bf16[2,512,1024]{1,2,0:T(8,128)(2,1)} collective-permute-done((bf16[2,512,1024]{1,2,0:T(8,128)(2,1)}, bf16[2,512,1024]{1,2,0:T(8,128)(2,1)}, u32[]{:S(2)}, u32[]{:S(2)}) %collective-permute-start.7) | collective-permute-done | bytes 2097184 | tf_op jit(solution)/shard_map/ppermute | solution.py:19
  306.1 6.3 %collective-permute-start.6 = (bf16[2,512,1024]{1,2,0:T(8,128)(2,1)}, bf16[2,512,1024]{1,2,0:T(8,128)(2,1)S(1)}, u32[]{:S(2)}, u32[]{:S(2)}) collective-permute-start(bf16[2,512,1024]{1,2,0:T(8,128)(2,1)} %pad_maximum_fusion), channel_id=1, source_target_pairs={{0,7},{1,8},{2,9},{3,10},{4,11},{5,12},{6,13},{7,14},{8,15},{16,23... | collective-permute-start | bytes 6291464 | tf_op jit(solution)/shard_map/ppermute | solution.py:19
  320.5 7.7 %fusion.18 = (f32[8,2,512]{2,1,0:T(2,128)S(1)}, f32[8,512,512,2]{2,1,3,0:T(8,128)}) fusion(pred[512,512]{0,1:T(8,128)(4,1)S(1)} %copy.55, bf16[512,8,128,1]{0,2,3,1:T(8,128)(2,1)S(1)} %bitcast.456, bf16[512,8,2,128]{3,2,1,0:T(2,128)(2,1)S(1)} %reshape.589), kind=kOutput, calls=%fused_computation.32 | convolution fusion | flops 1086316544 | bytes 20217856 | tf_op jit(solution)/shard_map/qhgd,khd->hgqk/dot_general | solution.py:64
  329.3 7.7 %fusion.24 = (f32[8,2,512]{2,1,0:T(2,128)S(1)}, f32[8,512,512,2]{2,1,3,0:T(8,128)}) fusion(pred[512,512]{0,1:T(8,128)(4,1)S(1)} %copy-done.4, bf16[512,8,128,1]{0,2,3,1:T(8,128)(2,1)S(1)} %bitcast.457, bf16[512,8,2,128]{3,2,1,0:T(2,128)(2,1)S(1)} %reshape.589), kind=kOutput, calls=%fused_computation.42 | convolution fusion | flops 1086316544 | bytes 20217856 | tf_op jit(solution)/shard_map/qhgd,khd->hgqk/dot_general | solution.py:64
  337.0 7.7 %fusion.3 = (f32[8,2,512]{2,1,0:T(2,128)S(1)}, f32[8,512,512,2]{2,1,3,0:T(8,128)}) fusion(pred[512,512]{0,1:T(8,128)(4,1)S(1)} %copy.70, bf16[512,8,128,1]{0,2,3,1:T(8,128)(2,1)S(1)} %bitcast.459, bf16[512,8,2,128]{3,2,1,0:T(2,128)(2,1)S(1)} %reshape.589), kind=kOutput, calls=%fused_computation.7 | convolution fusion | flops 1086316544 | bytes 20217856 | tf_op jit(solution)/shard_map/qhgd,khd->hgqk/dot_general | solution.py:64
  344.8 7.7 %fusion.9 = (f32[8,2,512]{2,1,0:T(2,128)S(1)}, f32[8,512,512,2]{2,1,3,0:T(8,128)}) fusion(pred[512,512]{0,1:T(8,128)(4,1)S(1)} %copy.64, bf16[512,8,128,1]{0,2,3,1:T(8,128)(2,1)S(1)} %bitcast.460, bf16[512,8,2,128]{3,2,1,0:T(2,128)(2,1)S(1)} %reshape.589), kind=kOutput, calls=%fused_computation.17 | convolution fusion | flops 1086316544 | bytes 20217856 | tf_op jit(solution)/shard_map/qhgd,khd->hgqk/dot_general | solution.py:64
  353.6 7.6 %fusion.12 = (f32[8,2,512]{2,1,0:T(2,128)S(1)}, f32[8,512,512,2]{2,1,3,0:T(8,128)}) fusion(pred[512,512]{0,1:T(8,128)(4,1)S(1)} %copy.61, bf16[512,8,128,1]{0,2,3,1:T(8,128)(2,1)S(1)} %bitcast.458, bf16[512,8,2,128]{3,2,1,0:T(2,128)(2,1)S(1)} %reshape.589), kind=kOutput, calls=%fused_computation.22 | convolution fusion | flops 1086316544 | bytes 20217856 | tf_op jit(solution)/shard_map/qhgd,khd->hgqk/dot_general | solution.py:64
  361.3 7.8 %fusion.15 = (f32[8,2,512]{2,1,0:T(2,128)S(1)}, f32[8,512,512,2]{2,1,3,0:T(8,128)}) fusion(pred[512,512]{0,1:T(8,128)(4,1)S(1)} %copy-done, bf16[512,8,128,1]{0,2,3,1:T(8,128)(2,1)S(1)} %bitcast.461, bf16[512,8,2,128]{3,2,1,0:T(2,128)(2,1)S(1)} %reshape.589), kind=kOutput, calls=%fused_computation.27 | convolution fusion | flops 1086316544 | bytes 20217856 | tf_op jit(solution)/shard_map/qhgd,khd->hgqk/dot_general | solution.py:64
  369.1 18.8 %fusion.21 = (f32[8,2,512]{2,1,0:T(2,128)S(1)}, f32[8,512,512,2]{2,1,3,0:T(8,128)}) fusion(pred[512,512]{0,1:T(8,128)(4,1)S(1)} %copy-done.2, bf16[512,8,128,1]{0,2,3,1:T(8,128)(2,1)S(1)} %bitcast.462, bf16[512,8,2,128]{3,2,1,0:T(2,128)(2,1)S(1)} %reshape.589), kind=kOutput, calls=%fused_computation.37 | convolution fusion | flops 1086316544 | bytes 20217856 | tf_op jit(solution)/shard_map/qhgd,khd->hgqk/dot_general | solution.py:64
  389.0 7.6 %fusion.6 = (f32[8,2,512]{2,1,0:T(2,128)S(1)}, f32[8,512,512,2]{2,1,3,0:T(8,128)}) fusion(pred[512,512]{0,1:T(8,128)(4,1)S(1)} %copy.67, bf16[512,8,128,1]{0,2,3,1:T(8,128)(2,1)S(1)} %bitcast.463, bf16[512,8,2,128]{3,2,1,0:T(2,128)(2,1)S(1)} %reshape.589), kind=kOutput, calls=%fused_computation.12 | convolution fusion | flops 1086316544 | bytes 20217856 | tf_op jit(solution)/shard_map/qhgd,khd->hgqk/dot_general | solution.py:64
  397.6 9.8 %fusion.33 = f32[8,2,512]{2,1,0:T(2,128)} fusion(f32[8,512,512,2]{2,1,3,0:T(8,128)} %get-tuple-element.121, f32[8,2,512]{2,1,0:T(2,128)S(1)} %get-tuple-element.86, pred[512,512]{0,1:T(8,128)(4,1)} %copy.47), kind=kLoop, calls=%fused_computation.53 | loop fusion | flops 16769024 | bytes 17104896 | tf_op jit(solution)/shard_map/reduce_sum | solution.py:71
  407.4 9.8 %fusion.35 = f32[8,2,512]{2,1,0:T(2,128)} fusion(f32[8,512,512,2]{2,1,3,0:T(8,128)} %get-tuple-element.119, f32[8,2,512]{2,1,0:T(2,128)S(1)} %get-tuple-element.85, pred[512,512]{0,1:T(8,128)(4,1)S(1)} %copy-done.3), kind=kLoop, calls=%fused_computation.55 | loop fusion | flops 16769024 | bytes 17104896 | tf_op jit(solution)/shard_map/reduce_sum | solution.py:71
  417.2 9.8 %fusion.37 = f32[8,2,512]{2,1,0:T(2,128)} fusion(f32[8,512,512,2]{2,1,3,0:T(8,128)} %get-tuple-element.117, f32[8,2,512]{2,1,0:T(2,128)S(1)} %get-tuple-element.84, pred[512,512]{0,1:T(8,128)(4,1)S(1)} %copy.55), kind=kLoop, calls=%fused_computation.57 | loop fusion | flops 16769024 | bytes 17104896 | tf_op jit(solution)/shard_map/reduce_sum | solution.py:71
  426.9 10.2 %fusion.39 = f32[8,2,512]{2,1,0:T(2,128)} fusion(f32[8,512,512,2]{2,1,3,0:T(8,128)} %get-tuple-element.115, f32[8,2,512]{2,1,0:T(2,128)S(1)} %get-tuple-element.83, pred[512,512]{0,1:T(8,128)(4,1)S(1)} %copy-done.1), kind=kLoop, calls=%fused_computation.59 | loop fusion | flops 16769024 | bytes 17104896 | tf_op jit(solution)/shard_map/reduce_sum | solution.py:71
  437.1 9.8 %fusion.41 = f32[8,2,512]{2,1,0:T(2,128)} fusion(f32[8,512,512,2]{2,1,3,0:T(8,128)} %get-tuple-element.113, f32[8,2,512]{2,1,0:T(2,128)S(1)} %get-tuple-element.82, pred[512,512]{0,1:T(8,128)(4,1)S(1)} %copy.61), kind=kLoop, calls=%fused_computation.61 | loop fusion | flops 16769024 | bytes 17104896 | tf_op jit(solution)/shard_map/reduce_sum | solution.py:71
  446.8 9.8 %fusion.43 = f32[8,2,512]{2,1,0:T(2,128)} fusion(f32[8,512,512,2]{2,1,3,0:T(8,128)} %get-tuple-element.111, f32[8,2,512]{2,1,0:T(2,128)S(1)} %get-tuple-element.81, pred[512,512]{0,1:T(8,128)(4,1)S(1)} %copy.64), kind=kLoop, calls=%fused_computation.63 | loop fusion | flops 16769024 | bytes 17104896 | tf_op jit(solution)/shard_map/reduce_sum | solution.py:71
  456.6 10.0 %fusion.47 = f32[8,2,512]{2,1,0:T(2,128)} fusion(f32[8,512,512,2]{2,1,3,0:T(8,128)} %get-tuple-element.107, f32[8,2,512]{2,1,0:T(2,128)S(1)} %get-tuple-element.79, pred[512,512]{0,1:T(8,128)(4,1)S(1)} %copy.70), kind=kLoop, calls=%fused_computation.67 | loop fusion | flops 16769024 | bytes 17104896 | tf_op jit(solution)/shard_map/reduce_sum | solution.py:71
  466.6 9.8 %fusion.45 = f32[8,2,512]{2,1,0:T(2,128)} fusion(f32[8,512,512,2]{2,1,3,0:T(8,128)} %get-tuple-element.109, f32[8,2,512]{2,1,0:T(2,128)S(1)} %get-tuple-element.80, pred[512,512]{0,1:T(8,128)(4,1)S(1)} %copy.67), kind=kLoop, calls=%fused_computation.65 | loop fusion | flops 16769024 | bytes 17104896 | tf_op jit(solution)/shard_map/reduce_sum | solution.py:71
  476.4 9.8 %fusion.31 = f32[8,2,512]{2,1,0:T(2,128)} fusion(f32[8,512,512,2]{2,1,3,0:T(8,128)} %get-tuple-element.123, f32[8,2,512]{2,1,0:T(2,128)S(1)} %get-tuple-element.105, pred[512,512]{0,1:T(8,128)(4,1)S(1)} %copy-done.6), kind=kLoop, calls=%fused_computation.51 | loop fusion | flops 16769024 | bytes 17104896 | tf_op jit(solution)/shard_map/reduce_sum | solution.py:71
  487.5 11.5 %fusion.62 = f32[8,2,512,128]{2,3,1,0:T(8,128)} fusion(bf16[512,8,128,1]{0,2,3,1:T(8,128)(2,1)} %bitcast.474, f32[8,512,512,2]{2,1,3,0:T(8,128)} %get-tuple-element.121, f32[8,2,512]{2,1,0:T(2,128)} %copy-done.35, pred[512,512]{0,1:T(8,128)(4,1)S(1)} %copy-done.5), kind=kOutput, calls=%fused_computation.75 | convolution fusion | flops 1090519040 | bytes 22315008 | tf_op jit(solution)/shard_map/hgqk,khd->hgqd/dot_general | solution.py:73
  499.0 11.6 %fusion.64 = f32[8,2,512,128]{2,3,1,0:T(8,128)} fusion(bf16[512,8,128,1]{0,2,3,1:T(8,128)(2,1)S(1)} %bitcast.467, f32[8,512,512,2]{2,1,3,0:T(8,128)} %get-tuple-element.123, f32[8,2,512]{2,1,0:T(2,128)S(1)} %copy-done.34, pred[512,512]{0,1:T(8,128)(4,1)S(1)} %copy-done.6), kind=kOutput, calls=%fused_computation.76 | convolution fusion | flops 1090519040 | bytes 22315008 | tf_op jit(solution)/shard_map/hgqk,khd->hgqd/dot_general | solution.py:73
  510.6 11.5 %fusion.60 = f32[8,2,512,128]{2,3,1,0:T(8,128)} fusion(bf16[512,8,128,1]{0,2,3,1:T(8,128)(2,1)S(1)} %bitcast.477, f32[8,512,512,2]{2,1,3,0:T(8,128)} %get-tuple-element.119, f32[8,2,512]{2,1,0:T(2,128)S(1)} %copy-done.32, pred[512,512]{0,1:T(8,128)(4,1)S(1)} %copy-done.3), kind=kOutput, calls=%fused_computation.74 | convolution fusion | flops 1090519040 | bytes 22315008 | tf_op jit(solution)/shard_map/hgqk,khd->hgqd/dot_general | solution.py:73
  522.2 5.3 fusion.58
  527.5 11.3 %fusion.56 = f32[8,2,512,128]{2,3,1,0:T(8,128)} fusion(bf16[512,8,128,1]{0,2,3,1:T(8,128)(2,1)S(1)} %bitcast.475, f32[8,512,512,2]{2,1,3,0:T(8,128)} %get-tuple-element.115, f32[8,2,512]{2,1,0:T(2,128)S(1)} %copy-done.28, pred[512,512]{0,1:T(8,128)(4,1)S(1)} %copy-done.1), kind=kOutput, calls=%fused_computation.72 | convolution fusion | flops 1090519040 | bytes 22315008 | tf_op jit(solution)/shard_map/hgqk,khd->hgqd/dot_general | solution.py:73
  538.8 11.4 %fusion.54 = f32[8,2,512,128]{2,3,1,0:T(8,128)} fusion(bf16[512,8,128,1]{0,2,3,1:T(8,128)(2,1)S(1)} %bitcast.473, f32[8,512,512,2]{2,1,3,0:T(8,128)} %get-tuple-element.113, f32[8,2,512]{2,1,0:T(2,128)S(1)} %copy-done.26, pred[512,512]{0,1:T(8,128)(4,1)S(1)} %copy.61), kind=kOutput, calls=%fused_computation.71 | convolution fusion | flops 1090519040 | bytes 22315008 | tf_op jit(solution)/shard_map/hgqk,khd->hgqd/dot_general | solution.py:73
  550.3 11.5 %fusion.52 = f32[8,2,512,128]{2,3,1,0:T(8,128)} fusion(bf16[512,8,128,1]{0,2,3,1:T(8,128)(2,1)S(1)} %bitcast.472, f32[8,512,512,2]{2,1,3,0:T(8,128)} %get-tuple-element.111, f32[8,2,512]{2,1,0:T(2,128)S(1)} %copy-done.24, pred[512,512]{0,1:T(8,128)(4,1)S(1)} %copy.64), kind=kOutput, calls=%fused_computation.70 | convolution fusion | flops 1090519040 | bytes 22315008 | tf_op jit(solution)/shard_map/hgqk,khd->hgqd/dot_general | solution.py:73
  561.8 11.5 %fusion.50 = f32[8,2,512,128]{2,3,1,0:T(8,128)} fusion(bf16[512,8,128,1]{0,2,3,1:T(8,128)(2,1)S(1)} %bitcast.476, f32[8,512,512,2]{2,1,3,0:T(8,128)} %get-tuple-element.109, f32[8,2,512]{2,1,0:T(2,128)S(1)} %copy-done.22, pred[512,512]{0,1:T(8,128)(4,1)S(1)} %copy.67), kind=kOutput, calls=%fused_computation.69 | convolution fusion | flops 1090519040 | bytes 22315008 | tf_op jit(solution)/shard_map/hgqk,khd->hgqd/dot_general | solution.py:73
  573.6 14.1 %fusion.104 = bf16[512,8,2,128]{0,3,2,1:T(8,128)(2,1)S(1)} fusion(f32[8,2,512,128]{2,3,1,0:T(8,128)} %fusion.50, f32[8,2,512,128]{2,3,1,0:T(8,128)} %fusion.52, f32[8,2,512,128]{2,3,1,0:T(8,128)} %fusion.54, f32[8,2,512,128]{2,3,1,0:T(8,128)} %fusion.56, f32[8,2,512,128]{2,3,1,0:T(8,128)} %fusion.58, f32[8,2,512,128]{2,3,1,0:T(8,128)} %fusion.60, ...), kind=kOutput, calls=%fused_computation.116 | convolution fusion | flops 1111490560 | bytes 54108160 | tf_op jit(solution)/shard_map/hgqk,khd->hgqd/dot_general | solution.py:73
  (261 shorter events, 96.3 us)
Async XLA Ops:
  1.5 63.5 %copy-start.7 = (bf16[512,1024]{0,1:T(8,128)(2,1)}, bf16[512,1024]{0,1:T(8,128)(2,1)S(1)}, u32[]{:S(2)}) copy-start(bf16[512,1024]{0,1:T(8,128)(2,1)S(1)} %copy.49) | copy-start | bytes 3145732
  4.9 85.8 %collective-permute-start.2 = (bf16[2,512,1024]{1,2,0:T(8,128)(2,1)}, bf16[2,512,1024]{1,2,0:T(8,128)(2,1)}, u32[]{:S(2)}, u32[]{:S(2)}) collective-permute-start(bf16[2,512,1024]{1,2,0:T(8,128)(2,1)} %pad_maximum_fusion), channel_id=1, source_target_pairs={{0,3},{1,4},{2,5},{3,6},{4,7},{5,8},{6,9},{7,10},{8,11},{9,12},{10... | collective-permute-start | bytes 6291464 | tf_op jit(solution)/shard_map/ppermute | solution.py:19
  12.3 93.6 %collective-permute-start = (bf16[2,512,1024]{1,2,0:T(8,128)(2,1)}, bf16[2,512,1024]{1,2,0:T(8,128)(2,1)}, u32[]{:S(2)}, u32[]{:S(2)}) collective-permute-start(bf16[2,512,1024]{1,2,0:T(8,128)(2,1)} %pad_maximum_fusion), channel_id=1, source_target_pairs={{0,1},{1,2},{2,3},{3,4},{4,5},{5,6},{6,7},{7,8},{8,9},{9,10},{10,1... | collective-permute-start | bytes 6291464 | tf_op jit(solution)/shard_map/ppermute | solution.py:19
  14.2 291.8 %collective-permute-start.7 = (bf16[2,512,1024]{1,2,0:T(8,128)(2,1)}, bf16[2,512,1024]{1,2,0:T(8,128)(2,1)}, u32[]{:S(2)}, u32[]{:S(2)}) collective-permute-start(bf16[2,512,1024]{1,2,0:T(8,128)(2,1)} %pad_maximum_fusion), channel_id=1, source_target_pairs={{0,8},{1,9},{2,10},{3,11},{4,12},{5,13},{6,14},{7,15},{16,24},{17,... | collective-permute-start | bytes 6291464 | tf_op jit(solution)/shard_map/ppermute | solution.py:19
  19.1 296.0 %collective-permute-start.5 = (bf16[2,512,1024]{1,2,0:T(8,128)(2,1)}, bf16[2,512,1024]{1,2,0:T(8,128)(2,1)}, u32[]{:S(2)}, u32[]{:S(2)}) collective-permute-start(bf16[2,512,1024]{1,2,0:T(8,128)(2,1)} %pad_maximum_fusion), channel_id=1, source_target_pairs={{0,6},{1,7},{2,8},{3,9},{4,10},{5,11},{6,12},{7,13},{8,14},{9,15},... | collective-permute-start | bytes 6291464 | tf_op jit(solution)/shard_map/ppermute | solution.py:19
  22.3 295.5 %collective-permute-start.4 = (bf16[2,512,1024]{1,2,0:T(8,128)(2,1)}, bf16[2,512,1024]{1,2,0:T(8,128)(2,1)}, u32[]{:S(2)}, u32[]{:S(2)}) collective-permute-start(bf16[2,512,1024]{1,2,0:T(8,128)(2,1)} %pad_maximum_fusion), channel_id=1, source_target_pairs={{0,5},{1,6},{2,7},{3,8},{4,9},{5,10},{6,11},{7,12},{8,13},{9,14},{... | collective-permute-start | bytes 6291464 | tf_op jit(solution)/shard_map/ppermute | solution.py:19
  90.7 237.4 %collective-permute-start.3 = (bf16[2,512,1024]{1,2,0:T(8,128)(2,1)}, bf16[2,512,1024]{1,2,0:T(8,128)(2,1)S(1)}, u32[]{:S(2)}, u32[]{:S(2)}) collective-permute-start(bf16[2,512,1024]{1,2,0:T(8,128)(2,1)} %pad_maximum_fusion), channel_id=1, source_target_pairs={{0,4},{1,5},{2,6},{3,7},{4,8},{5,9},{6,10},{7,11},{8,12},{9,13},{1... | collective-permute-start | bytes 6291464 | tf_op jit(solution)/shard_map/ppermute | solution.py:19
  105.9 246.6 %collective-permute-start.1 = (bf16[2,512,1024]{1,2,0:T(8,128)(2,1)}, bf16[2,512,1024]{1,2,0:T(8,128)(2,1)S(1)}, u32[]{:S(2)}, u32[]{:S(2)}) collective-permute-start(bf16[2,512,1024]{1,2,0:T(8,128)(2,1)} %pad_maximum_fusion), channel_id=1, source_target_pairs={{0,2},{1,3},{2,4},{3,5},{4,6},{5,7},{6,8},{7,9},{8,10},{9,11},{10,... | collective-permute-start | bytes 6291464 | tf_op jit(solution)/shard_map/ppermute | solution.py:19
  306.1 81.9 %collective-permute-start.6 = (bf16[2,512,1024]{1,2,0:T(8,128)(2,1)}, bf16[2,512,1024]{1,2,0:T(8,128)(2,1)S(1)}, u32[]{:S(2)}, u32[]{:S(2)}) collective-permute-start(bf16[2,512,1024]{1,2,0:T(8,128)(2,1)} %pad_maximum_fusion), channel_id=1, source_target_pairs={{0,7},{1,8},{2,9},{3,10},{4,11},{5,12},{6,13},{7,14},{8,15},{16,23... | collective-permute-start | bytes 6291464 | tf_op jit(solution)/shard_map/ppermute | solution.py:19
  352.5 44.9 %copy-start.16 = (f32[8,2,512]{2,1,0:T(2,128)}, f32[8,2,512]{2,1,0:T(2,128)S(1)}, u32[]{:S(2)}) copy-start(f32[8,2,512]{2,1,0:T(2,128)S(1)} %get-tuple-element.110) | copy-start | bytes 98308
  361.3 36.1 %copy-start.17 = (f32[8,2,512]{2,1,0:T(2,128)}, f32[8,2,512]{2,1,0:T(2,128)S(1)}, u32[]{:S(2)}) copy-start(f32[8,2,512]{2,1,0:T(2,128)S(1)} %get-tuple-element.112) | copy-start | bytes 98308
  397.5 19.7 %copy-start.31 = (f32[8,2,512]{2,1,0:T(2,128)}, f32[8,2,512]{2,1,0:T(2,128)S(1)}, u32[]{:S(2)}) copy-start(f32[8,2,512]{2,1,0:T(2,128)S(1)} %get-tuple-element.85) | copy-start | bytes 98308
  397.5 19.7 %copy-start.29 = (f32[8,2,512]{2,1,0:T(2,128)}, f32[8,2,512]{2,1,0:T(2,128)S(1)}, u32[]{:S(2)}) copy-start(f32[8,2,512]{2,1,0:T(2,128)S(1)} %get-tuple-element.84) | copy-start | bytes 98308
  397.5 29.4 %copy-start.27 = (f32[8,2,512]{2,1,0:T(2,128)}, f32[8,2,512]{2,1,0:T(2,128)S(1)}, u32[]{:S(2)}) copy-start(f32[8,2,512]{2,1,0:T(2,128)S(1)} %get-tuple-element.83) | copy-start | bytes 98308
  397.5 39.6 %copy-start.25 = (f32[8,2,512]{2,1,0:T(2,128)}, f32[8,2,512]{2,1,0:T(2,128)S(1)}, u32[]{:S(2)}) copy-start(f32[8,2,512]{2,1,0:T(2,128)S(1)} %get-tuple-element.82) | copy-start | bytes 98308
  397.5 49.3 %copy-start.23 = (f32[8,2,512]{2,1,0:T(2,128)}, f32[8,2,512]{2,1,0:T(2,128)S(1)}, u32[]{:S(2)}) copy-start(f32[8,2,512]{2,1,0:T(2,128)S(1)} %get-tuple-element.81) | copy-start | bytes 98308
  397.5 59.1 %copy-start.19 = (f32[8,2,512]{2,1,0:T(2,128)}, f32[8,2,512]{2,1,0:T(2,128)S(1)}, u32[]{:S(2)}) copy-start(f32[8,2,512]{2,1,0:T(2,128)S(1)} %get-tuple-element.79) | copy-start | bytes 98308
  397.6 69.0 %copy-start.21 = (f32[8,2,512]{2,1,0:T(2,128)}, f32[8,2,512]{2,1,0:T(2,128)S(1)}, u32[]{:S(2)}) copy-start(f32[8,2,512]{2,1,0:T(2,128)S(1)} %get-tuple-element.80) | copy-start | bytes 98308
  397.6 78.8 %copy-start.33 = (f32[8,2,512]{2,1,0:T(2,128)}, f32[8,2,512]{2,1,0:T(2,128)S(1)}, u32[]{:S(2)}) copy-start(f32[8,2,512]{2,1,0:T(2,128)S(1)} %get-tuple-element.105) | copy-start | bytes 98308
  407.4 19.6 %copy-start.1 = (pred[512,512]{0,1:T(8,128)(4,1)S(1)}, pred[512,512]{0,1:T(8,128)(4,1)}, u32[]{:S(2)}) copy-start(pred[512,512]{0,1:T(8,128)(4,1)} %copy.58) | copy-start | bytes 786436
  456.6 19.8 %copy-start.6 = (pred[512,512]{0,1:T(8,128)(4,1)S(1)}, pred[512,512]{0,1:T(8,128)(4,1)}, u32[]{:S(2)}) copy-start(pred[512,512]{0,1:T(8,128)(4,1)} %copy.44) | copy-start | bytes 786436
  466.6 20.9 %copy-start.5 = (pred[512,512]{0,1:T(8,128)(4,1)S(1)}, pred[512,512]{0,1:T(8,128)(4,1)}, u32[]{:S(2)}) copy-start(pred[512,512]{0,1:T(8,128)(4,1)} %copy.47) | copy-start | bytes 786436
  486.1 12.8 %copy-start.8 = (bf16[512,1024]{0,1:T(8,128)(2,1)S(1)}, bf16[512,1024]{0,1:T(8,128)(2,1)}, u32[]{:S(2)}) copy-start(bf16[512,1024]{0,1:T(8,128)(2,1)} %copy-done.7) | copy-start | bytes 3145732
  486.1 12.8 %copy-start.34 = (f32[8,2,512]{2,1,0:T(2,128)S(1)}, f32[8,2,512]{2,1,0:T(2,128)}, u32[]{:S(2)}) copy-start(f32[8,2,512]{2,1,0:T(2,128)} %copy-done.33) | copy-start | bytes 98308
  498.9 11.7 %copy-start.15 = (bf16[1,512,1024]{1,2,0:T(8,128)(2,1)S(1)}, bf16[1,512,1024]{1,2,0:T(8,128)(2,1)}, u32[]{:S(2)}) copy-start(bf16[1,512,1024]{1,2,0:T(8,128)(2,1)} %get-tuple-element.91) | copy-start | bytes 3145732
  498.9 11.7 %copy-start.32 = (f32[8,2,512]{2,1,0:T(2,128)S(1)}, f32[8,2,512]{2,1,0:T(2,128)}, u32[]{:S(2)}) copy-start(f32[8,2,512]{2,1,0:T(2,128)} %copy-done.31) | copy-start | bytes 98308
  499.0 23.2 %slice-start.4 = ((s8[16777216]{0:T(1024)(128)(4,1)}), s8[4194304]{0:T(1024)(128)(4,1)S(1)}, s32[]{:S(2)}) async-start(s8[16777216]{0:T(1024)(128)(4,1)} %bitcast.454), calls=%async_computation.4 | async-start | bytes 8388608
  499.0 23.2 %slice-start.5 = ((s8[16777216]{0:T(1024)(128)(4,1)}), s8[4194304]{0:T(1024)(128)(4,1)S(1)}, s32[]{:S(2)}) async-start(s8[16777216]{0:T(1024)(128)(4,1)} %bitcast.454), calls=%async_computation.5 | async-start | bytes 8388608
  550.3 23.0 %slice-start = ((s8[16777216]{0:T(1024)(128)(4,1)}), s8[4194304]{0:T(1024)(128)(4,1)S(1)}, s32[]{:S(2)}) async-start(s8[16777216]{0:T(1024)(128)(4,1)} %bitcast.452), calls=%async_computation | async-start | bytes 8388608
  550.3 23.0 %slice-start.1 = ((s8[16777216]{0:T(1024)(128)(4,1)}), s8[4194304]{0:T(1024)(128)(4,1)S(1)}, s32[]{:S(2)}) async-start(s8[16777216]{0:T(1024)(128)(4,1)} %bitcast.452), calls=%async_computation.1 | async-start | bytes 8388608
  561.8 11.8 %slice-start.2 = ((s8[16777216]{0:T(1024)(128)(4,1)}), s8[4194304]{0:T(1024)(128)(4,1)S(1)}, s32[]{:S(2)}) async-start(s8[16777216]{0:T(1024)(128)(4,1)} %bitcast.452), calls=%async_computation.2 | async-start | bytes 8388608
  561.8 11.8 %slice-start.3 = ((s8[16777216]{0:T(1024)(128)(4,1)}), s8[4194304]{0:T(1024)(128)(4,1)S(1)}, s32[]{:S(2)}) async-start(s8[16777216]{0:T(1024)(128)(4,1)} %bitcast.452), calls=%async_computation.3 | async-start | bytes 8388608
  (22 other events, 217.4 us)
where the time goes:
time: 601 us; the launch traced here: 591 us
  waiting for transfers between devices  196 us (33%)
  matrix products  191 us (32%)
  other arithmetic  123 us (20%)
  starting transfers between devices  40.2 us (7%)
  local copies, waits for them, and re-layouts  38.5 us (6%)
    ppermute x8, waiting for transfers between devices, passed_along(): return lax.ppermute(value, axis, pairs)  196 us
    dot_general x9, matrix products, attend(): jnp.einsum('hgqk,khd->hgqd', weights, value_heads, preferred_element_type...  99.6 us
    reduce_sum x9, other arithmetic, attend(): row_total = row_total * rescale + jnp.sum(exp_terms, axis=-1)  88.5 us
    dot_general x9, matrix products, attend(): jnp.einsum('qhgd,khd->hgqk', query_heads, key_heads, preferred_element_ty...  81.4 us
    ppermute x8, starting transfers between devices, passed_along(): return lax.ppermute(value, axis, pairs)  40.2 us
    reduce_sum x32, other arithmetic, advance(): current = jnp.sum(jnp.where(onehot, parents[None, :], 0), axis=1)  26.6 us
    slice x7, local copies, waits for them, and re-layouts, body(): arrived[1]  15.7 us
  transfers between devices with their start and end apart: 8, of which 1 were waited for; matrix products, arithmetic and copies ran while one was open for 25% of the time, Pallas kernels for 0%

commit v1 on v0

v1 whole, which is shorter than its diff:
```python
import functools

import jax
import jax.numpy as jnp
from jax import lax
from jax.experimental import pallas as pl
from jax.experimental.pallas import tpu as pltpu
from jax.sharding import PartitionSpec as P

HEADS = 16
KV_HEADS = 8
HEAD_DIM = 128
WINDOW = 4096
BLK = 128
TILES_DEV = 4
SLOTS = 2
ROW = 8
BLOCKS = 64
GROUP = 2 * HEAD_DIM
CHUNK = 4
NEG = -1e30
SCALE = 1.4426950408889634 / 12.0
MESH = pl.DeviceIdType.MESH


def place():
    c = lax.axis_index("ctx")
    return c, c // ROW, c % ROW


def peer(row, r):
    return {"ctx": row * ROW + r}


def spread_kernel(
    kept_ref, q_hbm, k_hbm, v_hbm, qg, kvg,
    q_v, k_v, v_v, qs, kvs, in_sem, kv_send, kv_recv, q_send, q_recv, up_send, up_recv, own_sem,
):
    c, row, r = place()
    loads = [
        pltpu.make_async_copy(k_hbm, k_v, in_sem.at[0]),
        pltpu.make_async_copy(v_hbm, v_v, in_sem.at[1]),
        pltpu.make_async_copy(q_hbm, q_v, in_sem.at[2]),
    ]
    for load in loads:
        load.start()
    barrier = pltpu.get_barrier_semaphore()
    for step in range(1, ROW):
        pl.semaphore_signal(barrier, 1, device_id=peer(row, (r + step) % ROW), device_id_type=MESH)
    pl.semaphore_signal(barrier, 1, device_id=peer(1 - row, r), device_id_type=MESH)

    f = [kept_ref[c * TILES_DEV + j] > 0 for j in range(TILES_DEV)]

    def pick(ref, slot, cols):
        t = [ref[j * BLK : (j + 1) * BLK, cols] for j in range(TILES_DEV)]
        if slot == 0:
            return jnp.where(f[0], t[0], jnp.where(f[1], t[1], jnp.where(f[2], t[2], t[3])))
        return jnp.where(f[3], t[3], jnp.where(f[2], t[2], jnp.where(f[1], t[1], t[0])))

    loads[0].wait()
    loads[1].wait()
    for slot in range(SLOTS):
        for h in range(ROW):
            cols = slice(h * HEAD_DIM, (h + 1) * HEAD_DIM)
            kvs[h, slot * BLK : (slot + 1) * BLK, :] = pick(k_v, slot, cols)
            kvs[h, (SLOTS + slot) * BLK : (SLOTS + slot + 1) * BLK, :] = pick(v_v, slot, cols)
    pl.semaphore_wait(barrier, ROW)

    def kv_copy(step):
        to = (r + step) % ROW
        return pltpu.make_async_remote_copy(
            kvs.at[to], kvg.at[ROW + r], kv_send.at[step], kv_recv.at[step],
            device_id=peer(row, to), device_id_type=MESH,
        )

    def q_copy(step):
        to = (r + step) % ROW
        return pltpu.make_async_remote_copy(
            qs.at[to], qg.at[r], q_send.at[step], q_recv.at[step],
            device_id=peer(row, to), device_id_type=MESH,
        )

    def up_copy(step):
        s = (r - step + ROW) % ROW
        src = kvs.at[r] if step == 0 else kvg.at[ROW + s]
        return pltpu.make_async_remote_copy(
            src, kvg.at[s], up_send.at[step], up_recv.at[step],
            device_id=peer(1 - row, r), device_id_type=MESH,
        )

    for step in range(1, ROW):
        kv_copy(step).start()

    @pl.when(row == 0)
    def _():
        up_copy(0).start()

    own_kv = pltpu.make_async_copy(kvs.at[r], kvg.at[ROW + r], own_sem.at[0])
    own_kv.start()
    loads[2].wait()
    for slot in range(SLOTS):
        for h in range(ROW):
            cols = slice(h * GROUP, (h + 1) * GROUP)
            qs[h, slot * BLK : (slot + 1) * BLK, :] = pick(q_v, slot, cols)
    own_q = pltpu.make_async_copy(qs.at[r], qg.at[r], own_sem.at[1])
    own_q.start()
    for step in range(1, ROW):
        kv_copy(step).wait_recv()

        @pl.when(row == 0)
        def _():
            up_copy(step).start()

        if step == 3:
            for other in range(1, ROW):
                q_copy(other).start()
    for step in range(1, ROW):
        q_copy(step).wait_recv()

    @pl.when(row == 1)
    def _():
        for step in range(ROW):
            up_copy(step).wait_recv()

    @pl.when(row == 0)
    def _():
        for step in range(ROW):
            up_copy(step).wait_send()

    for step in range(1, ROW):
        kv_copy(step).wait_send()
        q_copy(step).wait_send()
    own_kv.wait()
    own_q.wait()


def spread(kept, q, k, v):
    rows = q.shape[0]
    anywhere = pl.BlockSpec(memory_space=pl.ANY)
    bf16 = jnp.bfloat16
    dma = pltpu.SemaphoreType.DMA
    return pl.pallas_call(
        spread_kernel,
        out_shape=(
            jax.ShapeDtypeStruct((ROW, SLOTS * BLK, GROUP), bf16),
            jax.ShapeDtypeStruct((2 * ROW, 2 * SLOTS * BLK, HEAD_DIM), bf16),
        ),
        in_specs=[pl.BlockSpec(memory_space=pltpu.SMEM), anywhere, anywhere, anywhere],
        out_specs=(anywhere, anywhere),
        scratch_shapes=[
            pltpu.VMEM((rows, HEADS * HEAD_DIM), bf16),
            pltpu.VMEM((rows, KV_HEADS * HEAD_DIM), bf16),
            pltpu.VMEM((rows, KV_HEADS * HEAD_DIM), bf16),
            pltpu.VMEM((ROW, SLOTS * BLK, GROUP), bf16),
            pltpu.VMEM((ROW, 2 * SLOTS * BLK, HEAD_DIM), bf16),
            dma((3,)), dma((ROW,)), dma((ROW,)), dma((ROW,)), dma((ROW,)), dma((ROW,)), dma((ROW,)), dma((2,)),
        ],
        compiler_params=pltpu.CompilerParams(
            collective_id=1, has_side_effects=True, vmem_limit_bytes=60 << 20
        ),
        name="spread",
    )(kept, q, k, v)


def attend_kernel(parents_ref, kept_ref, qg, kvg, og, up_ref, base_ref, list_ref):
    c, row, r = place()
    end = BLOCKS
    first_tile = row * ROW * TILES_DEV

    up_ref[end] = -BLOCKS * 4
    up_ref[0] = end

    def link(t, _):
        p = parents_ref[t]
        up_ref[t] = jnp.where(kept_ref[p] > 0, p, up_ref[p])
        return 0

    lax.fori_loop(1, BLOCKS, link, 0)

    def locate(s, _):
        before = jnp.int32(0)
        lin = jnp.clip(s - ROW * row + ROW, 0, 2 * ROW - 1)
        for j in range(TILES_DEV):
            t = s * TILES_DEV + j
            base_ref[t] = lin * (2 * SLOTS * BLK) + jnp.minimum(before, SLOTS - 1) * BLK
            before = before + jnp.where(kept_ref[t] > 0, 1, 0)
        return 0

    lax.fori_loop(0, BLOCKS // TILES_DEV, locate, 0)
    base_ref[end] = ROW * 2 * SLOTS * BLK

    def collect(j, count):
        t = first_tile + j
        list_ref[count] = t
        return count + jnp.where(kept_ref[t] > 0, 1, 0)

    count = lax.fori_loop(0, ROW * TILES_DEV, collect, jnp.int32(0))
    rc = lax.broadcasted_iota(jnp.int32, (BLK, BLK), 0) - lax.broadcasted_iota(jnp.int32, (BLK, BLK), 1)
    rc = jnp.concatenate([rc, rc], 0)

    def pair(i, _):
        tiles = [list_ref[2 * i], list_ref[jnp.minimum(2 * i + 1, count - 1)]]
        at = []
        for t in tiles:
            slot = (base_ref[t] // BLK) % SLOTS
            at.append(((t - first_tile) // TILES_DEV, pl.multiple_of(slot * BLK, BLK)))
        heads = []
        for s, a in at:
            q = qg[s, pl.ds(a, BLK), :]
            heads.append(jnp.concatenate([q[:, :HEAD_DIM], q[:, HEAD_DIM:]], 0))

        def more(state):
            return (state[0] >= 0) | (state[1] >= 0)

        def step(state):
            nodes = list(state[:2])
            out = []
            for n in range(2):
                m, l, acc = state[2 + 3 * n : 5 + 3 * n]
                node = nodes[n]
                keys, values, gaps = [], [], []
                for _ in range(CHUNK):
                    ok = node >= 0
                    safe = jnp.where(ok, node, end)
                    base = pl.multiple_of(base_ref[safe], BLK)
                    keys.append(kvg[pl.ds(base, BLK), :])
                    values.append(kvg[pl.ds(base + SLOTS * BLK, BLK), :])
                    gaps.append(jnp.where(ok, (tiles[n] - node) * BLK, -WINDOW))
                    nxt = up_ref[safe]
                    node = jnp.where((nxt < end) & (nxt >= tiles[n] - WINDOW // BLK), nxt, -1)
                nodes[n] = node
                s = lax.dot_general(
                    heads[n], jnp.concatenate(keys, 0), (((1,), (1,)), ((), ())),
                    preferred_element_type=jnp.float32,
                ) * SCALE
                parts = []
                for g in range(CHUNK):
                    gap = rc + gaps[g]
                    fine = (gap >= 0) & (gap < WINDOW)
                    parts.append(jnp.where(fine, s[:, g * BLK : (g + 1) * BLK], NEG))
                top = functools.reduce(jnp.maximum, parts)
                new = jnp.maximum(m, jnp.max(top, axis=1, keepdims=True))
                shrink = jnp.exp2(m - new)
                terms = [jnp.exp2(part - new) for part in parts]
                l = l * shrink + sum(terms)
                w = jnp.concatenate([term.astype(jnp.bfloat16) for term in terms], 1)
                acc = acc * shrink + jnp.dot(
                    w, jnp.concatenate(values, 0), preferred_element_type=jnp.float32
                )
                out += [new, l, acc]
            return (*nodes, *out)

        start = []
        for _ in range(2):
            start += [
                jnp.full((2 * BLK, 1), NEG, jnp.float32),
                jnp.zeros((2 * BLK, BLK), jnp.float32),
                jnp.zeros((2 * BLK, HEAD_DIM), jnp.float32),
            ]
        end_state = lax.while_loop(more, step, (tiles[0], tiles[1], *start))
        for n in range(2):
            _, l, acc = end_state[2 + 3 * n : 5 + 3 * n]
            total = jnp.sum(l, axis=1, keepdims=True)
            o = (acc / total).astype(jnp.bfloat16)
            s, a = at[n]
            og[s, pl.ds(a, BLK), :] = jnp.concatenate([o[:BLK], o[BLK:]], 1)
        return 0

    lax.fori_loop(0, (count + 1) // 2, pair, 0)


def attend(parents, kept, qg, kvg):
    smem = pl.BlockSpec(memory_space=pltpu.SMEM)
    vmem = pl.BlockSpec(memory_space=pltpu.VMEM)
    return pl.pallas_call(
        attend_kernel,
        out_shape=jax.ShapeDtypeStruct((ROW, SLOTS * BLK, GROUP), jnp.bfloat16),
        in_specs=[smem, smem, vmem, vmem],
        out_specs=vmem,
        scratch_shapes=[
            pltpu.SMEM((BLOCKS + 1,), jnp.int32),
            pltpu.SMEM((BLOCKS + 1,), jnp.int32),
            pltpu.SMEM((ROW * TILES_DEV + 1,), jnp.int32),
        ],
        compiler_params=pltpu.CompilerParams(vmem_limit_bytes=32 << 20),
        name="attend",
    )(parents, kept, qg, kvg.reshape(2 * ROW * 2 * SLOTS * BLK, HEAD_DIM))


def collect_kernel(og, oc, send, recv, own_sem):
    _, row, r = place()
    barrier = pltpu.get_barrier_semaphore()
    for step in range(1, ROW):
        pl.semaphore_signal(barrier, 1, device_id=peer(row, (r + step) % ROW), device_id_type=MESH)
    own = pltpu.make_async_copy(og.at[r], oc.at[r], own_sem)
    own.start()
    pl.semaphore_wait(barrier, ROW - 1)
    copies = []
    for step in range(1, ROW):
        to = (r + step) % ROW
        copies.append(
            pltpu.make_async_remote_copy(
                og.at[to], oc.at[r], send.at[step], recv.at[step],
                device_id=peer(row, to), device_id_type=MESH,
            )
        )
    for copy in copies:
        copy.start()
    for copy in copies:
        copy.wait_recv()
    for copy in copies:
        copy.wait_send()
    own.wait()


def collect(og):
    anywhere = pl.BlockSpec(memory_space=pl.ANY)
    vmem = pl.BlockSpec(memory_space=pltpu.VMEM)
    return pl.pallas_call(
        collect_kernel,
        out_shape=jax.ShapeDtypeStruct((ROW, SLOTS * BLK, GROUP), jnp.bfloat16),
        in_specs=[vmem],
        out_specs=vmem,
        scratch_shapes=[
            pltpu.SemaphoreType.DMA((ROW,)), pltpu.SemaphoreType.DMA((ROW,)), pltpu.SemaphoreType.DMA,
        ],
        compiler_params=pltpu.CompilerParams(collective_id=2, has_side_effects=True),
        name="collect",
    )(og)


def expand_kernel(kept_ref, oc, out, wide, sem):
    c, _, _ = place()
    copies = []
    before = jnp.bool_(False)
    for j in range(TILES_DEV):
        rows = slice(j * BLK, (j + 1) * BLK)
        kept = kept_ref[c * TILES_DEV + j] > 0
        slot = pl.multiple_of(jnp.where(before, BLK, 0), BLK)

        @pl.when(kept)
        def _():
            for h in range(ROW):
                wide[rows, h * GROUP : (h + 1) * GROUP] = oc[h, pl.ds(slot, BLK), :]

        @pl.when(jnp.logical_not(kept))
        def _():
            wide[rows, :] = jnp.zeros((BLK, HEADS * HEAD_DIM), jnp.bfloat16)

        before = before | kept
        copies.append(pltpu.make_async_copy(wide.at[rows], out.at[rows], sem.at[j]))
        copies[-1].start()
    for copy in copies:
        copy.wait()


def expand(kept, oc):
    rows = TILES_DEV * BLK
    return pl.pallas_call(
        expand_kernel,
        out_shape=jax.ShapeDtypeStruct((rows, HEADS * HEAD_DIM), jnp.bfloat16),
        in_specs=[pl.BlockSpec(memory_space=pltpu.SMEM), pl.BlockSpec(memory_space=pltpu.VMEM)],
        out_specs=pl.BlockSpec(memory_space=pl.ANY),
        scratch_shapes=[
            pltpu.VMEM((rows, HEADS * HEAD_DIM), jnp.bfloat16), pltpu.SemaphoreType.DMA((TILES_DEV,)),
        ],
        name="expand",
    )(kept, oc)


def body(queries, key_rows, value_rows, parents, kept_tiles):
    qg, kvg = spread(kept_tiles, queries, key_rows, value_rows)
    og = attend(parents, kept_tiles, qg, kvg)
    return expand(kept_tiles, collect(og))


def solution(mesh):
    return jax.shard_map(
        body,
        mesh=mesh,
        in_specs=(
            P(("dp", "ctx"), None),
            P(("dp", "ctx"), None),
            P(("dp", "ctx"), None),
            P("dp"),
            P("dp"),
        ),
        out_specs=P(("dp", "ctx"), None),
        check_vma=False,
    )
```

time: 601 us -> 69.5 us (0.12)
  the two profiles are of different devices: /device:TPU:1 before, /device:TPU:81 now
where the time goes in v1:
time: 69.5 us; the launch traced here: 69.3 us
  Pallas kernels  65.4 us (94%)
  local copies, waits for them, and re-layouts  3.78 us (5%)
    pallas_call x1, Pallas kernels, spread(): pl.pallas_call(spread_kernel, out_shape=(jax.ShapeDtypeStruct((ROW, SLOTS...  30.9 us
    pallas_call x1, Pallas kernels, collect(): pl.pallas_call(collect_kernel, out_shape=jax.ShapeDtypeStruct((ROW, SLOTS...  18.1 us
    pallas_call x1, Pallas kernels, attend(): pl.pallas_call(attend_kernel, out_shape=jax.ShapeDtypeStruct((ROW, SLOTS...  13.8 us
    unnamed x10, local copies, waits for them, and re-layouts  3.78 us
    pallas_call x1, Pallas kernels, expand(): pl.pallas_call(expand_kernel, out_shape=jax.ShapeDtypeStruct((rows, HEADS...  2.63 us

profile of v1, /device:TPU:81, one launch (start us, length us, event | category | flops | bytes accessed | tf_op | source)
XLA Modules:
  0.0 69.3 jit_solution(6397438251806459033)
XLA Ops:
  0.0 0.0 copy-start.3
  0.0 0.0 copy-start.4
  0.0 30.9 %spread.1 = (bf16[8,256,256]{2,1,0:T(8,128)(2,1)}, bf16[16,512,128]{2,1,0:T(8,128)(2,1)}) custom-call(s32[64]{0:T(128)} %kept_ref.5, bf16[512,2048]{1,0:T(8,128)(2,1)} %q_hbm.1, bf16[512,1024]{1,0:T(8,128)(2,1)} %k_hbm.1, bf16[512,1024]{1,0:T(8,128)(2,1)} %v_hbm.1), custom_call_target="tpu_custom_call" | custom-call | tf_op jit(solution)/shard_map/spread/pallas_call | solution.py:142
  30.9 0.0 copy-done.3
  30.9 0.0 copy-done.4
  30.9 0.0 copy-start.1
  30.9 1.6 %copy-done.1 = bf16[16,512,128]{2,1,0:T(8,128)(2,1)S(1)} copy-done((bf16[16,512,128]{2,1,0:T(8,128)(2,1)S(1)}, bf16[16,512,128]{2,1,0:T(8,128)(2,1)}, u32[]{:S(2)}) %copy-start.1) | copy-done | bytes 2097176
  32.5 0.0 copy-start.2
  32.5 1.2 %copy-done.2 = bf16[8,256,256]{2,1,0:T(8,128)(2,1)S(1)} copy-done((bf16[8,256,256]{2,1,0:T(8,128)(2,1)S(1)}, bf16[8,256,256]{2,1,0:T(8,128)(2,1)}, u32[]{:S(2)}) %copy-start.2) | copy-done | bytes 1048600
  33.7 13.8 %attend.1.og = bf16[8,256,256]{2,1,0:T(8,128)(2,1)S(1)} custom-call(s32[64]{0:T(128)S(1)} %copy-done.4, s32[64]{0:T(128)S(1)} %copy-done.3, bf16[8,256,256]{2,1,0:T(8,128)(2,1)S(1)} %copy-done.2, bf16[8192,128]{1,0:T(8,128)(2,1)S(1)} %bitcast.1), custom_call_target="tpu_custom_call" | custom-call | tf_op jit(solution)/shard_map/attend/pallas_call | solution.py:275
  47.5 0.0 copy-start
  47.6 1.0 %copy-done = bf16[8,256,256]{2,1,0:T(8,128)(2,1)} copy-done((bf16[8,256,256]{2,1,0:T(8,128)(2,1)}, bf16[8,256,256]{2,1,0:T(8,128)(2,1)S(1)}, u32[]{:S(2)}) %copy-start) | copy-done | bytes 1048600
  48.5 18.1 %collect.1.oc = bf16[8,256,256]{2,1,0:T(8,128)(2,1)} custom-call(bf16[8,256,256]{2,1,0:T(8,128)(2,1)} %copy-done), custom_call_target="tpu_custom_call" | custom-call | tf_op jit(solution)/shard_map/collect/pallas_call | solution.py:319
  66.6 2.6 %expand.1 = bf16[512,2048]{1,0:T(8,128)(2,1)} custom-call(s32[64]{0:T(128)} %kept_ref.5, bf16[8,256,256]{2,1,0:T(8,128)(2,1)} %collect.1.oc), custom_call_target="tpu_custom_call" | custom-call | tf_op jit(solution)/shard_map/expand/pallas_call | solution.py:359
Async XLA Ops:
  0.0 30.9 %copy-start.3 = (s32[64]{0:T(128)S(1)}, s32[64]{0:T(128)}, u32[]{:S(2)}) copy-start(s32[64]{0:T(128)} %kept_ref.5) | copy-start | bytes 772
  0.0 30.9 %copy-start.4 = (s32[64]{0:T(128)S(1)}, s32[64]{0:T(128)}, u32[]{:S(2)}) copy-start(s32[64]{0:T(128)} %parents_ref.1) | copy-start | bytes 772
  30.9 1.6 %copy-start.1 = (bf16[16,512,128]{2,1,0:T(8,128)(2,1)S(1)}, bf16[16,512,128]{2,1,0:T(8,128)(2,1)}, u32[]{:S(2)}) copy-start(bf16[16,512,128]{2,1,0:T(8,128)(2,1)} %get-tuple-element.8) | copy-start | bytes 6291460
  32.5 1.2 %copy-start.2 = (bf16[8,256,256]{2,1,0:T(8,128)(2,1)S(1)}, bf16[8,256,256]{2,1,0:T(8,128)(2,1)}, u32[]{:S(2)}) copy-start(bf16[8,256,256]{2,1,0:T(8,128)(2,1)} %get-tuple-element.7.qg) | copy-start | bytes 3145732
  47.5 1.0 %copy-start = (bf16[8,256,256]{2,1,0:T(8,128)(2,1)}, bf16[8,256,256]{2,1,0:T(8,128)(2,1)S(1)}, u32[]{:S(2)}) copy-start(bf16[8,256,256]{2,1,0:T(8,128)(2,1)S(1)} %attend.1.og) | copy-start | bytes 3145732
